TPU v7x, 128 devices: a whole 4x4x4 slice. The times are simulated.
128 devices in a mesh: row: 8 (over x_lo, z), col: 16 (over x_hi, y, core).
Axes of the slice: x: 4 (x_hi: 2, x_lo: 2; x = x_hi * 2 + x_lo), y: 4, z: 4, core: 2. Of those that a mesh axis runs over, the one named last changes fastest.
Arguments:
- level_set: float32 [384, 384, 384], P('col', 'row'), may hold values from -7 to 7
- image: float32 [384, 384, 384], P('col', 'row'), may hold values from -6 to 6
Outputs:
- updated_level: float32 [384, 384, 384], P('col', 'row')
All inputs are finite; a program needn't handle non-finite values.
Results may differ from a plain program's by a relative error of at most 0.00021.
Values sent between devices are 32-bit elements; how exact they have to be, the bound alone decides.
A program may use at most 128 MiB of HBM per device.

v0:
```python
import jax
import jax.numpy as jnp
from jax import lax
from jax.sharding import PartitionSpec as P

RADIUS = 6
sigma_cells = 8.0
dt_step = 0.5
nu_diff = 0.1
eps_fit = 0.05


def extended(value, sides, width):
    for axis, dim in sides:
        devices, length = (lax.axis_size(axis), value.shape[dim])
        up = [(i, (i + 1) % devices) for i in range(devices)]
        down = [(j, i) for i, j in up]
        last = lax.slice_in_dim(value, length - width, length, axis=dim)
        first = lax.slice_in_dim(value, 0, width, axis=dim)
        before = lax.ppermute(last, axis, up)
        after = lax.ppermute(first, axis, down)
        value = jnp.concatenate([before, value, after], axis=dim)
    return value


def tap_weight(offset):
    tap_offsets = lax.iota(jnp.int32, 2 * RADIUS + 1) - RADIUS
    tap_float = tap_offsets.astype(jnp.float32)
    total_weight = jnp.sum(jnp.exp(-tap_float * tap_float / (2.0 * sigma_cells * sigma_cells)))
    off_float = offset.astype(jnp.float32)
    inside = jnp.abs(offset) <= RADIUS
    weights = jnp.where(
        inside, jnp.exp(-off_float * off_float / (2.0 * sigma_cells * sigma_cells)), 0.0
    )
    return weights / total_weight


def gauss_table(length):
    indices = lax.iota(jnp.int32, length)
    distance = jnp.abs(indices[:, None] - indices[None, :])
    distance = jnp.minimum(distance, length - distance)
    return tap_weight(distance)


def lines_along_x(fields, kernel_table):
    along_x = jnp.einsum("fzyx,xw->fwzy", fields, kernel_table, precision=lax.Precision.HIGHEST)
    return along_x.reshape(4, fields.shape[3], fields.shape[1] * fields.shape[2])


def fit_coeffs(smoothed):
    first, second, third, fourth = (smoothed[0], smoothed[1], smoothed[2], smoothed[3])
    inside_mean = first / (second + eps_fit)
    outside_mean = (third - first) / (1.0 - second + eps_fit)
    spread = fourth - third * third + eps_fit
    slope_term = 2.0 * (inside_mean - outside_mean) / spread
    offset = (outside_mean * outside_mean - inside_mean * inside_mean) / spread
    return jnp.stack([slope_term, offset])


def body(level_set, image):
    highest = lax.Precision.HIGHEST
    z_local, y_local, length = level_set.shape
    n_row = lax.axis_size("row")
    kernel_table = gauss_table(length)
    heaviside = 0.5 + jnp.arctan(level_set) / jnp.pi
    fields = jnp.stack([heaviside * image, heaviside, image, image * image])
    along_x = lines_along_x(fields, kernel_table)
    row_table = kernel_table.reshape(n_row, y_local, length)
    x_local = length // n_row
    received = lax.all_to_all(along_x, "row", split_axis=1, concat_axis=2, tiled=True)
    received = received.reshape(4, x_local, n_row, z_local, y_local)
    along_y = jnp.einsum("fwrzy,ryv->fwzv", received, row_table, precision=highest)
    received_z = lax.all_to_all(along_y, "col", split_axis=3, concat_axis=2, tiled=True)
    along_z = jnp.einsum("fxzy,zw->fxyw", received_z, kernel_table, precision=highest)
    coeffs = fit_coeffs(along_z)
    returned = lax.all_to_all(coeffs, "col", split_axis=3, concat_axis=2, tiled=True)
    returned = lax.all_to_all(returned, "row", split_axis=2, concat_axis=1, tiled=True)
    local_coeffs = jnp.transpose(returned, (0, 3, 2, 1))
    forcing = image * local_coeffs[0] + local_coeffs[1]
    padded = extended(level_set, (("row", 1), ("col", 0)), 1)
    laplace = (
        padded[2:, 1:-1, :]
        + padded[:-2, 1:-1, :]
        + padded[1:-1, 2:, :]
        + padded[1:-1, :-2, :]
        + jnp.roll(level_set, 1, 2)
        + jnp.roll(level_set, -1, 2)
        - 6.0 * level_set
    )
    dirac_weight = 1.0 / (jnp.pi * (1.0 + level_set * level_set))
    return level_set + dt_step * (nu_diff * laplace + dirac_weight * forcing)


def solution(mesh):
    return jax.shard_map(
        body,
        mesh=mesh,
        in_specs=(P("col", "row", None), P("col", "row", None)),
        out_specs=P("col", "row", None),
        check_vma=False,
    )
```

profile of v0, /device:TPU:25, one launch (start us, length us, event | category | flops | bytes accessed | tf_op | source)
XLA Modules:
  0.0 704.8 jit_solution(235425075818692739)
XLA Ops:
  4.9 16.5 %fusion = f32[384,4,24,48]{0,3,2,1:T(8,128)} fusion(f32[1,24,48,384]{3,2,1,0:T(8,128)S(1)} %get-tuple-element.17, f32[1,24,48,384]{3,2,1,0:T(8,128)S(1)} %bitcast.87, f32[1,24,48,384]{3,2,1,0:T(8,128)S(1)} %get-tuple-element.16, f32[1,24,48,384]{3,2,1,0:T(8,128)S(1)} %get-tuple-element.15, f32[]{:T(128)} %fusion.59), kind=kOutput, calls=%fused_computation | convolution fusion | flops 8160804864 | bytes 14155780 | tf_op jit(solution)/shard_map/fzyx,xw->fwzy/dot_general | solution.py:46
  21.4 10.1 %copy.27 = f32[4,384,1152]{2,0,1:T(4,128)} copy(f32[4,384,1152]{1,2,0:T(8,128)} %bitcast.86) | data formatting | bytes 14155776 | tf_op jit(solution)/shard_map/reshape | solution.py:47
  38.0 79.6 %all-to-all-done = f32[4,384,1152]{2,0,1:T(4,128)} async-done(((f32[4,384,1152]{2,0,1:T(4,128)}), f32[4,384,1152]{2,0,1:T(4,128)}, u32[]{:S(2)}, u32[]{:S(2)}) %all-to-all-start) | async-done | bytes 7077920 | tf_op jit(solution)/shard_map/all_to_all | solution.py:70
  126.1 15.1 %reshape.71 = f32[4,48,8,24,48]{4,3,2,1,0:T(8,128)} reshape(f32[4,48,8,1152]{3,2,1,0:T(8,128)} %copy.29) | data formatting | bytes 14155776 | tf_op jit(solution)/shard_map/reshape | solution.py:71
  141.2 22.0 %convolution_bitcast_fusion = f32[4,48,24,384]{3,2,1,0:T(8,128)} fusion(f32[4,48,8,24,48]{4,3,2,1,0:T(8,128)} %reshape.71, f32[]{:T(128)} %fusion.59, s32[8,48]{1,0:T(8,128)S(1)} %multiply_add_fusion.1), kind=kOutput, calls=%fused_computation.9 | convolution fusion | flops 8155496448 | bytes 14157316 | tf_op jit(solution)/shard_map/fwrzy,ryv->fwzv/dot_general | solution.py:72
  163.2 17.4 %copy.30 = f32[4,48,24,384]{1,2,0,3:T(8,128)} copy(f32[4,48,24,384]{3,2,1,0:T(8,128)} %convolution_bitcast_fusion) | data formatting | bytes 14155776 | tf_op jit(solution)/shard_map/fwrzy,ryv->fwzv/dot_general | solution.py:72
  180.6 22.5 %reshape.75 = f32[16,1,110592]{2,1,0:T(1,128)} reshape(f32[384,4,24,48]{3,2,1,0:T(8,128)} %bitcast.76) | data formatting | bytes 14155776
  203.1 88.3 %all_to_all.69 = f32[16,1,110592]{2,1,0:T(1,128)} all-to-all(f32[16,1,110592]{2,1,0:T(1,128)} %reshape.75), channel_id=1, replica_groups=mesh['row'=8,'col'=16] {'col'}, dimensions={0} | all-to-all | bytes 14155776 | tf_op jit(solution)/shard_map/all_to_all | solution.py:73
  292.0 76.7 %reduce = f32[16,110592]{1,0:T(8,128)} reduce(f32[16,1,110592]{2,1,0:T(1,128)} %all_to_all.69, f32[]{:T(128)} %broadcast.153), dimensions={1}, to_apply=%all_to_all.53.reduce_sub_computation | reduce | bytes 14155780 | tf_op jit(solution)/shard_map/all_to_all | solution.py:73
  368.7 18.8 %reshape.76 = f32[384,4,24,48]{3,2,1,0:T(8,128)} reshape(f32[16,110592]{1,0:T(8,128)} %reduce) | data formatting | bytes 14155776
  387.5 15.8 %copy.32 = f32[4,48,16,24,24]{1,4,3,2,0:T(8,128)} copy(f32[4,48,16,24,24]{1,3,0,4,2:T(8,128)} %bitcast.77) | data formatting | bytes 14155776 | tf_op jit(solution)/shard_map/all_to_all | solution.py:73
  403.3 14.5 %copy.33 = f32[4,48,384,24]{2,3,1,0:T(8,128)} copy(f32[4,48,384,24]{1,3,2,0:T(8,128)} %bitcast.78) | data formatting | bytes 14155776 | tf_op jit(solution)/shard_map/all_to_all | solution.py:73
  417.8 19.2 %fusion.38 = f32[4,48,24,384]{3,2,1,0:T(8,128)S(1)} fusion(f32[4,48,384,24]{2,3,1,0:T(8,128)} %copy.33, f32[]{:T(128)} %fusion.59), kind=kOutput, calls=%fused_computation.63 | convolution fusion | flops 8155496448 | bytes 14155780 | tf_op jit(solution)/shard_map/fxzy,zw->fxyw/dot_general | solution.py:74
  444.1 15.2 %reshape.77 = f32[16,1,55296]{2,1,0:T(1,128)} reshape(f32[384,2,24,48]{3,2,1,0:T(8,128)} %bitcast.79) | data formatting | bytes 7077888
  459.3 48.5 %all_to_all.70 = f32[16,1,55296]{2,1,0:T(1,128)S(1)} all-to-all(f32[16,1,55296]{2,1,0:T(1,128)} %reshape.77), channel_id=1, replica_groups=mesh['row'=8,'col'=16] {'col'}, dimensions={0} | all-to-all | bytes 7077888 | tf_op jit(solution)/shard_map/all_to_all | solution.py:76
  507.8 30.2 %reduce.1 = f32[16,55296]{1,0:T(8,128)} reduce(f32[16,1,55296]{2,1,0:T(1,128)S(1)} %all_to_all.70, f32[]{:T(128)} %broadcast.153), dimensions={1}, to_apply=%all_to_all.57.reduce_sub_computation | reduce | bytes 7077892 | tf_op jit(solution)/shard_map/all_to_all | solution.py:76
  538.0 11.1 %reshape.78 = f32[384,2,24,48]{3,2,1,0:T(8,128)} reshape(f32[16,55296]{1,0:T(8,128)} %reduce.1) | data formatting | bytes 7077888
  549.1 6.7 copy.36
  560.2 12.1 %reshape.79 = f32[8,1,110592]{2,1,0:T(1,128)} reshape(f32[384,2,24,48]{3,2,1,0:T(8,128)} %bitcast.82) | data formatting | bytes 7077888
  582.4 37.7 %collective-permute-done = f32[24,1,384]{2,1,0:T(1,128)S(1)} collective-permute-done((f32[24,1,384]{2,1,0:T(1,128)S(1)}, f32[24,1,384]{2,1,0:T(1,128)S(1)}, u32[]{:S(2)}, u32[]{:S(2)}) %collective-permute-start) | collective-permute-done | bytes 36896 | tf_op jit(solution)/shard_map/ppermute | solution.py:20
  628.0 39.6 %reduce.2 = f32[8,110592]{1,0:T(8,128)} reduce(f32[8,1,110592]{2,1,0:T(1,128)} %all-to-all-done.3, f32[]{:T(128)} %broadcast.153), dimensions={1}, to_apply=%all_to_all.61.reduce_sub_computation | reduce | bytes 7077892 | tf_op jit(solution)/shard_map/all_to_all | solution.py:77
  667.6 9.4 %reshape.80 = f32[384,2,24,48]{3,2,1,0:T(8,128)} reshape(f32[8,110592]{1,0:T(8,128)} %reduce.2) | data formatting | bytes 7077888
  677.0 12.8 %copy.39 = f32[2,8,48,48,24]{2,1,3,4,0:T(8,128)} copy(f32[2,8,48,48,24]{2,4,0,3,1:T(8,128)} %bitcast.83) | data formatting | bytes 7077888 | tf_op jit(solution)/shard_map/all_to_all | solution.py:77
  689.8 8.3 %all_to_all.64 = f32[2,384,48,24]{1,2,3,0:T(8,128)} reshape(f32[2,8,48,48,24]{2,1,3,4,0:T(8,128)} %copy.39) | data formatting | bytes 7077888 | tf_op jit(solution)/shard_map/all_to_all | solution.py:77
  (33 shorter events, 56.2 us)
Async XLA Ops:
  0.6 4.3 copy-start.1
  31.5 86.1 %all-to-all-start = ((f32[4,384,1152]{2,0,1:T(4,128)}), f32[4,384,1152]{2,0,1:T(4,128)}, u32[]{:S(2)}, u32[]{:S(2)}) async-start(f32[4,384,1152]{2,0,1:T(4,128)} %copy.27), calls=%async_computation | async-start | bytes 14155776 | tf_op jit(solution)/shard_map/all_to_all | solution.py:70
  572.3 4.6 copy-start
  572.3 55.6 %all-to-all-start.3 = ((f32[8,1,110592]{2,1,0:T(1,128)}), f32[8,1,110592]{2,1,0:T(1,128)}, u32[]{:S(2)}, u32[]{:S(2)}) async-start(f32[8,1,110592]{2,1,0:T(1,128)} %reshape.79), calls=%async_computation.3 | async-start | bytes 7077888 | tf_op jit(solution)/shard_map/all_to_all | solution.py:77
  577.0 43.1 %collective-permute-start = (f32[24,1,384]{2,1,0:T(1,128)S(1)}, f32[24,1,384]{2,1,0:T(1,128)S(1)}, u32[]{:S(2)}, u32[]{:S(2)}) collective-permute-start(f32[24,1,384]{2,1,0:T(1,128)S(1)} %get-tuple-element.14), channel_id=1, source_target_pairs={{0,16},{16,32},{32,48},{48,64},{64,80},{80,96},{96,112},{112,0},{1... | collective-permute-start | bytes 110600 | tf_op jit(solution)/shard_map/ppermute | solution.py:20
  578.4 41.7 %collective-permute-start.1 = (f32[24,1,384]{2,1,0:T(1,128)S(1)}, f32[24,1,384]{2,1,0:T(1,128)S(1)}, u32[]{:S(2)}, u32[]{:S(2)}) collective-permute-start(f32[24,1,384]{2,1,0:T(1,128)S(1)} %get-tuple-element.13), channel_id=1, source_target_pairs={{16,0},{32,16},{48,32},{64,48},{80,64},{96,80},{112,96},{0,112},{1... | collective-permute-start | bytes 110600 | tf_op jit(solution)/shard_map/ppermute | solution.py:21
  620.1 0.6 copy-start.2
  620.7 0.7 copy-start.3
  621.4 76.7 %collective-permute-start.2 = (f32[1,50,384]{2,1,0:T(8,128)}, f32[1,50,384]{2,1,0:T(8,128)}, u32[]{:S(2)}, u32[]{:S(2)}) collective-permute-start(f32[1,50,384]{2,1,0:T(8,128)} %get-tuple-element.7), channel_id=1, source_target_pairs={{1,0},{2,1},{3,2},{4,3},{5,4},{6,5},{7,6},{8,7},{9,8},{10,9},{11,1... | collective-permute-start | bytes 230408 | tf_op jit(solution)/shard_map/ppermute | solution.py:21
  622.7 75.4 %collective-permute-start.3 = (f32[1,50,384]{2,1,0:T(8,128)}, f32[1,50,384]{2,1,0:T(8,128)}, u32[]{:S(2)}, u32[]{:S(2)}) collective-permute-start(f32[1,50,384]{2,1,0:T(8,128)} %get-tuple-element.8), channel_id=1, source_target_pairs={{0,1},{1,2},{2,3},{3,4},{4,5},{5,6},{6,7},{7,8},{8,9},{9,10},{10,1... | collective-permute-start | bytes 230408 | tf_op jit(solution)/shard_map/ppermute | solution.py:20
where the time goes:
time: 715 us; the launch traced here: 705 us
  local copies, waits for them, and re-layouts  213 us (30%)
  other arithmetic  160 us (22%)
  blocking collectives  137 us (19%)
  waiting for transfers between devices  117 us (16%)
  matrix products  57.7 us (8%)
  starting transfers between devices  20.1 us (3%)
    unnamed x14, local copies, waits for them, and re-layouts  89.8 us
    all_to_all x1, blocking collectives, body(): lax.all_to_all(along_y, 'col', split_axis=3, concat_axis=2, tiled=True)  88.3 us
    all_to_all x1, waiting for transfers between devices, body(): lax.all_to_all(along_x, 'row', split_axis=1, concat_axis=2, tiled=True)  79.6 us
    all_to_all x1, other arithmetic, body(): lax.all_to_all(along_y, 'col', split_axis=3, concat_axis=2, tiled=True)  76.7 us
    all_to_all x1, blocking collectives, body(): lax.all_to_all(coeffs, 'col', split_axis=3, concat_axis=2, tiled=True)  48.5 us
    all_to_all x1, other arithmetic, body(): lax.all_to_all(returned, 'row', split_axis=2, concat_axis=1, tiled=True)  39.6 us
    ppermute x2, waiting for transfers between devices, extended(): before = lax.ppermute(last, axis, up)  37.7 us
    all_to_all x3, local copies, waits for them, and re-layouts, body(): lax.all_to_all(along_y, 'col', split_axis=3, concat_axis=2, tiled=True)  30.8 us
  transfers between devices with their start and end apart: 6, of which 2 were waited for; matrix products, arithmetic and copies ran while one was open for 9% of the time, Pallas kernels for 0%

commit v1 on v0

--- a/solution.py
+++ b/solution.py
@@ -70,7 +70,10 @@
     received = lax.all_to_all(along_x, "row", split_axis=1, concat_axis=2, tiled=True)
     received = received.reshape(4, x_local, n_row, z_local, y_local)
     along_y = jnp.einsum("fwrzy,ryv->fwzv", received, row_table, precision=highest)
-    received_z = lax.all_to_all(along_y, "col", split_axis=3, concat_axis=2, tiled=True)
+    item_now = lax.all_to_all(
+        jnp.stack(jnp.split(along_y, lax.psum(1, "col"), 3), axis=0), "col", 0, 0
+    )
+    received_z = jnp.concatenate(item_now, 2)
     along_z = jnp.einsum("fxzy,zw->fxyw", received_z, kernel_table, precision=highest)
     coeffs = fit_coeffs(along_z)
     returned = lax.all_to_all(coeffs, "col", split_axis=3, concat_axis=2, tiled=True)

time: 715 us -> 759 us (1.062)
  local copies, waits for them, and re-layouts: 213 us -> 257 us
    another operation x0 -> x2, local copies, waits for them, and re-layouts: none -> 32.5 us  [body(): jnp.stack(jnp.split(along_y, lax.psum(1, 'col'), 3), axis=0)]
    unnamed x14 -> x29, local copies, waits for them, and re-layouts: 89.8 us -> 121 us
    all_to_all x3 -> x1, local copies, waits for them, and re-layouts: 30.8 us -> 0.59 us  [body(): lax.all_to_all(jnp.stack(jnp.split(along_y, lax.psum(1, 'col'), 3), axis=...]
    reshape x0 -> x3, local copies, waits for them, and re-layouts: none -> 28.6 us  [body(): received_z = jnp.concatenate(item_now, 2)]
    dot_general x1 -> x0, local copies, waits for them, and re-layouts: 17.4 us -> none  [body(): jnp.einsum('fwrzy,ryv->fwzv', received, row_table, precision=highest)]
where the time goes in v1:
time: 759 us; the launch traced here: 749 us
  local copies, waits for them, and re-layouts  257 us (34%)
  other arithmetic  160 us (21%)
  blocking collectives  137 us (18%)
  waiting for transfers between devices  117 us (15%)
  matrix products  57.5 us (8%)
  starting transfers between devices  19.8 us (3%)
    unnamed x29, local copies, waits for them, and re-layouts  121 us
    all_to_all x1, blocking collectives, body(): lax.all_to_all(jnp.stack(jnp.split(along_y, lax.psum(1, 'col'), 3), axis=...  88.3 us
    all_to_all x1, waiting for transfers between devices, body(): lax.all_to_all(along_x, 'row', split_axis=1, concat_axis=2, tiled=True)  79.6 us
    all_to_all x1, other arithmetic, body(): lax.all_to_all(jnp.stack(jnp.split(along_y, lax.psum(1, 'col'), 3), axis=...  76.7 us
    all_to_all x1, blocking collectives, body(): lax.all_to_all(coeffs, 'col', split_axis=3, concat_axis=2, tiled=True)  48.5 us
    all_to_all x1, other arithmetic, body(): lax.all_to_all(returned, 'row', split_axis=2, concat_axis=1, tiled=True)  39.6 us
    ppermute x2, waiting for transfers between devices, extended(): before = lax.ppermute(last, axis, up)  37.7 us
    another operation x2, local copies, waits for them, and re-layouts, body(): jnp.stack(jnp.split(along_y, lax.psum(1, 'col'), 3), axis=0)  32.5 us
  transfers between devices with their start and end apart: 6, of which 2 were waited for; matrix products, arithmetic and copies ran while one was open for 9% of the time, Pallas kernels for 0%

profile of v1, /device:TPU:25, one launch (start us, length us, event | category | flops | bytes accessed | tf_op | source)
XLA Modules:
  0.0 748.7 jit_solution(17188797253840994411)
XLA Ops:
  4.9 16.5 %fusion = f32[384,4,24,48]{0,3,2,1:T(8,128)} fusion(f32[1,24,48,384]{3,2,1,0:T(8,128)S(1)} %get-tuple-element.17, f32[1,24,48,384]{3,2,1,0:T(8,128)S(1)} %bitcast.150, f32[1,24,48,384]{3,2,1,0:T(8,128)S(1)} %get-tuple-element.16, f32[1,24,48,384]{3,2,1,0:T(8,128)S(1)} %get-tuple-element.15, f32[]{:T(128)} %fusion.75), kind=kOutput, calls=%fused_computation | convolution fusion | flops 8160804864 | bytes 14155780 | tf_op jit(solution)/shard_map/fzyx,xw->fwzy/dot_general | solution.py:46
  21.4 10.1 %copy.24 = f32[4,384,1152]{2,0,1:T(4,128)} copy(f32[4,384,1152]{1,2,0:T(8,128)} %bitcast.149) | data formatting | bytes 14155776 | tf_op jit(solution)/shard_map/reshape | solution.py:47
  37.7 79.6 %all-to-all-done = f32[4,384,1152]{2,0,1:T(4,128)} async-done(((f32[4,384,1152]{2,0,1:T(4,128)}), f32[4,384,1152]{2,0,1:T(4,128)}, u32[]{:S(2)}, u32[]{:S(2)}) %all-to-all-start) | async-done | bytes 7077920 | tf_op jit(solution)/shard_map/all_to_all | solution.py:70
  125.9 15.1 %reshape.77 = f32[4,48,8,24,48]{4,3,2,1,0:T(8,128)} reshape(f32[4,48,8,1152]{3,2,1,0:T(8,128)} %copy.26) | data formatting | bytes 14155776 | tf_op jit(solution)/shard_map/reshape | solution.py:71
  140.9 21.7 %convolution_bitcast_fusion = f32[4,48,24,384]{3,2,1,0:T(8,128)S(1)} fusion(f32[4,48,8,24,48]{4,3,2,1,0:T(8,128)} %reshape.77, f32[]{:T(128)} %fusion.75, s32[8,48]{1,0:T(8,128)S(1)} %multiply_add_fusion.1), kind=kOutput, calls=%fused_computation.9 | convolution fusion | flops 8155496448 | bytes 14157316 | tf_op jit(solution)/shard_map/fwrzy,ryv->fwzv/dot_general | solution.py:72
  195.9 30.4 %copy.27 = f32[16,4,48,24,24]{2,4,3,1,0:T(8,128)} copy(f32[16,4,48,24,24]{4,3,2,1,0:T(8,128)} %fusion.8) | data formatting | bytes 14155776 | tf_op jit(solution)/shard_map/stack | solution.py:74
  226.2 22.5 %reshape.83 = f32[16,1,110592]{2,1,0:T(1,128)} reshape(f32[16,4,24,24,48]{4,3,2,1,0:T(8,128)} %bitcast.140) | data formatting | bytes 14155776
  248.7 88.3 %all_to_all.56 = f32[16,1,110592]{2,1,0:T(1,128)} all-to-all(f32[16,1,110592]{2,1,0:T(1,128)} %reshape.83), channel_id=1, replica_groups=mesh['row'=8,'col'=16] {'col'}, dimensions={0} | all-to-all | bytes 14155776 | tf_op jit(solution)/shard_map/all_to_all | solution.py:73
  337.6 76.7 %reduce = f32[16,110592]{1,0:T(8,128)} reduce(f32[16,1,110592]{2,1,0:T(1,128)} %all_to_all.56, f32[]{:T(128)} %broadcast.153), dimensions={1}, to_apply=%all_to_all.43.reduce_sub_computation | reduce | bytes 14155780 | tf_op jit(solution)/shard_map/all_to_all | solution.py:73
  414.2 18.8 %reshape.84 = f32[16,4,24,24,48]{4,3,2,1,0:T(8,128)} reshape(f32[16,110592]{1,0:T(8,128)} %reduce) | data formatting | bytes 14155776
  433.1 7.3 bitcast_bitcast_fusion
  440.4 6.9 copy.28
  447.3 14.4 %copy.29 = f32[4,48,384,24]{2,3,1,0:T(8,128)} copy(f32[4,48,384,24]{1,3,2,0:T(8,128)} %bitcast.141) | data formatting | bytes 14155776 | tf_op jit(solution)/shard_map/reshape | solution.py:76
  461.7 19.2 %fusion.54 = f32[4,48,24,384]{3,2,1,0:T(8,128)S(1)} fusion(f32[4,48,384,24]{2,3,1,0:T(8,128)} %copy.29, f32[]{:T(128)} %fusion.75), kind=kOutput, calls=%fused_computation.95 | convolution fusion | flops 8155496448 | bytes 14155780 | tf_op jit(solution)/shard_map/fxzy,zw->fxyw/dot_general | solution.py:77
  488.0 15.2 %reshape.85 = f32[16,1,55296]{2,1,0:T(1,128)} reshape(f32[384,2,24,48]{3,2,1,0:T(8,128)} %bitcast.142) | data formatting | bytes 7077888
  503.2 48.5 %all_to_all.57 = f32[16,1,55296]{2,1,0:T(1,128)S(1)} all-to-all(f32[16,1,55296]{2,1,0:T(1,128)} %reshape.85), channel_id=1, replica_groups=mesh['row'=8,'col'=16] {'col'}, dimensions={0} | all-to-all | bytes 7077888 | tf_op jit(solution)/shard_map/all_to_all | solution.py:79
  551.7 30.2 %reduce.1 = f32[16,55296]{1,0:T(8,128)} reduce(f32[16,1,55296]{2,1,0:T(1,128)S(1)} %all_to_all.57, f32[]{:T(128)} %broadcast.153), dimensions={1}, to_apply=%all_to_all.44.reduce_sub_computation | reduce | bytes 7077892 | tf_op jit(solution)/shard_map/all_to_all | solution.py:79
  581.9 11.1 %reshape.86 = f32[384,2,24,48]{3,2,1,0:T(8,128)} reshape(f32[16,55296]{1,0:T(8,128)} %reduce.1) | data formatting | bytes 7077888
  604.1 12.1 %reshape.87 = f32[8,1,110592]{2,1,0:T(1,128)} reshape(f32[384,2,24,48]{3,2,1,0:T(8,128)} %bitcast.145) | data formatting | bytes 7077888
  626.4 37.7 %collective-permute-done = f32[24,1,384]{2,1,0:T(1,128)S(1)} collective-permute-done((f32[24,1,384]{2,1,0:T(1,128)S(1)}, f32[24,1,384]{2,1,0:T(1,128)S(1)}, u32[]{:S(2)}, u32[]{:S(2)}) %collective-permute-start) | collective-permute-done | bytes 36896 | tf_op jit(solution)/shard_map/ppermute | solution.py:20
  671.9 39.6 %reduce.2 = f32[8,110592]{1,0:T(8,128)} reduce(f32[8,1,110592]{2,1,0:T(1,128)} %all-to-all-done.3, f32[]{:T(128)} %broadcast.153), dimensions={1}, to_apply=%all_to_all.48.reduce_sub_computation | reduce | bytes 7077892 | tf_op jit(solution)/shard_map/all_to_all | solution.py:80
  711.5 9.4 %reshape.88 = f32[384,2,24,48]{3,2,1,0:T(8,128)} reshape(f32[8,110592]{1,0:T(8,128)} %reduce.2) | data formatting | bytes 7077888
  720.9 12.8 %copy.35 = f32[2,8,48,48,24]{2,1,3,4,0:T(8,128)} copy(f32[2,8,48,48,24]{2,4,0,3,1:T(8,128)} %bitcast.146) | data formatting | bytes 7077888 | tf_op jit(solution)/shard_map/all_to_all | solution.py:80
  733.7 8.3 %all_to_all.51 = f32[2,384,48,24]{1,2,3,0:T(8,128)} reshape(f32[2,8,48,48,24]{2,1,3,4,0:T(8,128)} %copy.35) | data formatting | bytes 7077888 | tf_op jit(solution)/shard_map/all_to_all | solution.py:80
  (50 shorter events, 95.8 us)
Async XLA Ops:
  0.6 4.3 copy-start.1
  31.5 85.8 %all-to-all-start = ((f32[4,384,1152]{2,0,1:T(4,128)}), f32[4,384,1152]{2,0,1:T(4,128)}, u32[]{:S(2)}, u32[]{:S(2)}) async-start(f32[4,384,1152]{2,0,1:T(4,128)} %copy.24), calls=%async_computation | async-start | bytes 14155776 | tf_op jit(solution)/shard_map/all_to_all | solution.py:70
  616.2 4.6 copy-start
  616.2 55.6 %all-to-all-start.3 = ((f32[8,1,110592]{2,1,0:T(1,128)}), f32[8,1,110592]{2,1,0:T(1,128)}, u32[]{:S(2)}, u32[]{:S(2)}) async-start(f32[8,1,110592]{2,1,0:T(1,128)} %reshape.87), calls=%async_computation.3 | async-start | bytes 7077888 | tf_op jit(solution)/shard_map/all_to_all | solution.py:80
  620.9 43.1 %collective-permute-start = (f32[24,1,384]{2,1,0:T(1,128)S(1)}, f32[24,1,384]{2,1,0:T(1,128)S(1)}, u32[]{:S(2)}, u32[]{:S(2)}) collective-permute-start(f32[24,1,384]{2,1,0:T(1,128)S(1)} %get-tuple-element.14), channel_id=1, source_target_pairs={{0,16},{16,32},{32,48},{48,64},{64,80},{80,96},{96,112},{112,0},{1... | collective-permute-start | bytes 110600 | tf_op jit(solution)/shard_map/ppermute | solution.py:20
  622.3 41.7 %collective-permute-start.1 = (f32[24,1,384]{2,1,0:T(1,128)S(1)}, f32[24,1,384]{2,1,0:T(1,128)S(1)}, u32[]{:S(2)}, u32[]{:S(2)}) collective-permute-start(f32[24,1,384]{2,1,0:T(1,128)S(1)} %get-tuple-element.13), channel_id=1, source_target_pairs={{16,0},{32,16},{48,32},{64,48},{80,64},{96,80},{112,96},{0,112},{1... | collective-permute-start | bytes 110600 | tf_op jit(solution)/shard_map/ppermute | solution.py:21
  664.0 0.6 copy-start.2
  664.6 0.7 copy-start.3
  665.3 76.7 %collective-permute-start.2 = (f32[1,50,384]{2,1,0:T(8,128)}, f32[1,50,384]{2,1,0:T(8,128)}, u32[]{:S(2)}, u32[]{:S(2)}) collective-permute-start(f32[1,50,384]{2,1,0:T(8,128)} %get-tuple-element.7), channel_id=1, source_target_pairs={{1,0},{2,1},{3,2},{4,3},{5,4},{6,5},{7,6},{8,7},{9,8},{10,9},{11,1... | collective-permute-start | bytes 230408 | tf_op jit(solution)/shard_map/ppermute | solution.py:21
  666.6 75.4 %collective-permute-start.3 = (f32[1,50,384]{2,1,0:T(8,128)}, f32[1,50,384]{2,1,0:T(8,128)}, u32[]{:S(2)}, u32[]{:S(2)}) collective-permute-start(f32[1,50,384]{2,1,0:T(8,128)} %get-tuple-element.8), channel_id=1, source_target_pairs={{0,1},{1,2},{2,3},{3,4},{4,5},{5,6},{6,7},{7,8},{8,9},{9,10},{10,1... | collective-permute-start | bytes 230408 | tf_op jit(solution)/shard_map/ppermute | solution.py:20
